TPU v7x, 256 devices: a whole 4x4x8 slice. The times are simulated.
256 devices in a mesh: cell: 8 (over z_hi, x), seq: 32 (over z_lo, y, core).
Axes of the slice: x: 4, y: 4, z: 8 (z_hi: 2, z_lo: 4; z = z_hi * 4 + z_lo), core: 2. Of those that a mesh axis runs over, the one named last changes fastest.
Arguments:
- features: bfloat16 [8192, 1536], P('seq', 'cell'), may hold values from -6 to 6
- w_qkv: bfloat16 [1536, 768], replicated, may hold values from -0.15625 to 0.15625
- buckets: int32 [8, 64, 16], P('cell', 'seq'), may hold values from 0 to 31
- cell_ids: int32 [8], P('cell'), may hold values from 0 to 31
- bias_table: float32 [32, 32, 2], replicated, may hold values from -8 to 330
- d_attended: bfloat16 [8, 8192, 256], P('cell', 'seq'), may hold values from -6 to 6
Outputs:
- attended: bfloat16 [8, 8192, 256], P('cell', 'seq')
- grad_qkv: float32 [1536, 768], P('cell')
- grad_table: float32 [32, 32, 2], replicated
All inputs are finite; a program needn't handle non-finite values.
Results may differ from a plain program's by a relative error of at most 0.02.
Values may be sent and summed in bfloat16 or wider, within the bound.
A program may use at most 64 MiB of HBM per device.

v0:
```python
import math
import jax
import jax.numpy as jnp
from jax import lax
from jax.sharding import PartitionSpec as P

HEADS = 2
HD = 128
TILE = 128
BT = 16


def passed_along(block, axis, distance):
    devices = range(lax.axis_size(axis))
    route = [(i - distance, i) for i in devices if i - distance in devices]
    return lax.ppermute(block, axis, route)


def tile_bias(bucket_rows, table_row, query_tiles, key_first, key_count, tile_total):
    band_width = bucket_rows.shape[1]
    middle = band_width // 2
    key_tiles = (key_first + jnp.arange(key_count, dtype=jnp.int32)) // TILE
    offsets = key_tiles[None, :] - query_tiles[:, None] + middle
    key_valid = (key_tiles >= 0) & (key_tiles < tile_total)
    query_valid = (query_tiles >= 0) & (query_tiles < tile_total)
    inside = (offsets >= 0) & (offsets < band_width) & key_valid[None, :] & query_valid[:, None]
    matches = offsets[:, :, None] == jnp.arange(band_width, dtype=jnp.int32)[None, None, :]
    bucket_ids = jnp.sum(jnp.where(matches, bucket_rows[:, None, :], 0), axis=2)
    levels = table_row.shape[0]
    onehot = (bucket_ids[:, :, None] == jnp.arange(levels, dtype=jnp.int32)[None, None, :]).astype(
        jnp.float32
    )
    bias_terms = jnp.einsum("qkb,bh->qhk", onehot, table_row, precision=lax.Precision.HIGHEST)
    return (bias_terms, inside, onehot)


def band_scores(query_rows, key_rows, bias_terms, inside, factor):
    raw_scores = jnp.einsum(
        "qhd,khd->qhk", query_rows, key_rows, preferred_element_type=jnp.float32
    )
    tile_count = bias_terms.shape[0]
    shaped = raw_scores.reshape(tile_count, TILE, raw_scores.shape[1], raw_scores.shape[2]) * factor
    shaped = shaped + bias_terms[:, None]
    keep_mask = jnp.broadcast_to(inside[:, None, None, :], shaped.shape)
    shaped = jnp.where(keep_mask, shaped, -1e30)
    return (shaped.reshape(raw_scores.shape), keep_mask.reshape(raw_scores.shape))


def fetch_keys(block, offset):
    return passed_along(block, "seq", -offset)


def return_grads(block, offset):
    return passed_along(block, "seq", offset)


def local(features, w_qkv, buckets, cell_ids, bias_table, d_attended):
    row_count = features.shape[0]
    width_part = features.shape[1]
    inner_width = HEADS * HD
    seq_count = lax.axis_size("seq")
    total_rows = row_count * seq_count
    tile_total = total_rows // TILE
    factor = 1.0 / math.sqrt(HD)
    seq_pos = lax.axis_index("seq")
    tiles_here = row_count // TILE
    half_band = BT * TILE // 2
    reach = min((half_band + row_count - 1) // row_count, seq_count - 1)
    span = 2 * reach + 1
    window_first = (seq_pos - reach) * row_count
    query_tiles = seq_pos * tiles_here + jnp.arange(tiles_here, dtype=jnp.int32)
    cell_pos = lax.axis_index("cell")
    weight_rows = lax.dynamic_slice_in_dim(w_qkv, cell_pos * width_part, width_part, 0)
    partial_qkv = jnp.dot(features, weight_rows, preferred_element_type=jnp.float32)
    projected = lax.psum(partial_qkv, "cell").astype(jnp.bfloat16)
    queries_flat = projected[:, :inner_width]
    queries = queries_flat.reshape(row_count, HEADS, HD)
    queries_wide = queries.astype(jnp.float32)
    key_value = projected[:, inner_width:]
    window_pieces = []
    for offset in range(-reach, reach + 1):
        if offset == 0:
            window_pieces.append(key_value)
        else:
            window_pieces.append(fetch_keys(key_value, offset))
    window_kv = jnp.concatenate(window_pieces, axis=0)
    window_keys = window_kv[:, :inner_width].reshape(span * row_count, HEADS, HD)
    window_values = window_kv[:, inner_width:].reshape(span * row_count, HEADS, HD)
    type_hit = jnp.arange(bias_table.shape[0], dtype=jnp.int32) == cell_ids[0]
    table_row = jnp.sum(jnp.where(type_hit[:, None, None], bias_table, 0.0), axis=0)
    bucket_rows = buckets[0]

    def block_terms(block_index):
        local_first = block_index * row_count
        key_blk = lax.dynamic_slice_in_dim(window_keys, local_first, row_count, 0)
        value_blk = lax.dynamic_slice_in_dim(window_values, local_first, row_count, 0)
        bias_terms, inside, onehot = tile_bias(
            bucket_rows, table_row, query_tiles, window_first + local_first, row_count, tile_total
        )
        scores, keep_mask = band_scores(queries, key_blk, bias_terms, inside, factor)
        return (key_blk, value_blk, scores, keep_mask, onehot)

    def stats_step(block_index, loop_carry):
        row_top, row_mass = loop_carry
        scores, keep_mask = block_terms(block_index)[2:4]
        new_top = jnp.maximum(row_top, jnp.max(scores, axis=2))
        fresh = jnp.sum(jnp.where(keep_mask, jnp.exp(scores - new_top[:, :, None]), 0.0), axis=2)
        return (new_top, row_mass * jnp.exp(row_top - new_top) + fresh)

    start_top = jnp.full((row_count, HEADS), -1e30, jnp.float32)
    start_mass = jnp.zeros((row_count, HEADS), jnp.float32)
    row_top, row_mass = lax.fori_loop(0, span, stats_step, (start_top, start_mass))
    log_total = row_top + jnp.log(row_mass)

    def value_step(block_index, value_sum):
        value_blk, scores, keep_mask = block_terms(block_index)[1:4]
        weights = jnp.where(keep_mask, jnp.exp(scores - log_total[:, :, None]), 0.0).astype(
            jnp.bfloat16
        )
        return value_sum + jnp.einsum(
            "qhk,khd->qhd", weights, value_blk, preferred_element_type=jnp.float32
        )

    value_sum = lax.fori_loop(0, span, value_step, jnp.zeros((row_count, HEADS, HD), jnp.float32))
    attended = value_sum.astype(jnp.bfloat16)
    grad_flat = d_attended[0]
    grad_out = grad_flat.reshape(row_count, HEADS, HD)
    row_delta = jnp.sum(grad_out.astype(jnp.float32) * attended.astype(jnp.float32), axis=2)
    levels = bias_table.shape[1]

    def grad_core(block_index):
        key_blk, value_blk, scores, keep_mask, onehot = block_terms(block_index)
        chance = jnp.where(keep_mask, jnp.exp(scores - log_total[:, :, None]), 0.0)
        chance_b = chance.astype(jnp.bfloat16)
        grad_push = jnp.einsum(
            "qhd,khd->qhk", grad_out, value_blk, preferred_element_type=jnp.float32
        )
        dscore = chance * (grad_push - row_delta[:, :, None])
        q_part = jnp.einsum(
            "qhk,khd->qhd",
            dscore,
            key_blk.astype(jnp.float32),
            precision=lax.Precision.HIGHEST,
            preferred_element_type=jnp.float32,
        )
        tile_sum = dscore.reshape(tiles_here, TILE, HEADS, row_count).sum(axis=1)
        table_part = jnp.einsum("qhk,qkb->bh", tile_sum, onehot, precision=lax.Precision.HIGHEST)
        return (chance_b, dscore, q_part, table_part)

    zero_rows = jnp.zeros((row_count, HEADS, HD), jnp.float32)
    zero_table = jnp.zeros((levels, HEADS), jnp.float32)

    def grad_step(block_index, loop_carry):
        q_total, table_total, key_store = loop_carry
        chance_b, dscore, q_part, table_part = grad_core(block_index)
        key_part = (
            jnp.einsum(
                "qhk,qhd->khd",
                dscore,
                queries_wide,
                precision=lax.Precision.HIGHEST,
                preferred_element_type=jnp.float32,
            )
            * factor
        )
        value_part = jnp.einsum(
            "qhk,qhd->khd", chance_b, grad_out, preferred_element_type=jnp.float32
        )
        merged = jnp.concatenate(
            [key_part.reshape(row_count, inner_width), value_part.reshape(row_count, inner_width)],
            axis=1,
        )
        key_store = lax.dynamic_update_slice_in_dim(key_store, merged, block_index * row_count, 0)
        return (q_total + q_part, table_total + table_part, key_store)

    key_store = jnp.zeros((span * row_count, 2 * inner_width), jnp.float32)
    q_total, table_total, key_store = lax.fori_loop(
        0, span, grad_step, (zero_rows, zero_table, key_store)
    )
    key_grads = key_store[reach * row_count : (reach + 1) * row_count]
    for slot_index in range(span):
        offset = slot_index - reach
        if offset != 0:
            segment = key_store[slot_index * row_count : (slot_index + 1) * row_count]
            key_grads = key_grads + return_grads(segment, offset)
    query_grads = (q_total * factor).reshape(row_count, inner_width)
    row_grads = jnp.concatenate([query_grads, key_grads], axis=1)
    summed_rows = lax.psum(row_grads, "cell")
    share = jnp.dot(
        features.astype(jnp.float32).T,
        summed_rows,
        precision=lax.Precision.HIGHEST,
        preferred_element_type=jnp.float32,
    )
    grad_qkv = lax.psum(share, "seq")
    table_term = jnp.where(type_hit[:, None, None], table_total[None, :, :], 0.0)
    grad_table = lax.psum(table_term, ("cell", "seq"))
    return (attended.reshape(1, row_count, inner_width), grad_qkv, grad_table)


def solution(mesh):
    in_specs = (
        P("seq", "cell"),
        P(),
        P("cell", "seq", None),
        P("cell"),
        P(),
        P("cell", "seq", None),
    )
    out_specs = (P("cell", "seq", None), P("cell", None), P())
    return jax.shard_map(local, mesh=mesh, in_specs=in_specs, out_specs=out_specs, check_vma=False)
```

profile of v0, /device:TPU:2, one launch (start us, length us, event | category | flops | bytes accessed | tf_op | source)
XLA Modules:
  0.0 758.4 jit_solution(12148896757726910611)
XLA Ops:
  7.3 1.6 copy-done
  10.0 63.3 %all-reduce.7 = bf16[256,768]{0,1:T(8,128)(2,1)} all-reduce(f32[256,768]{0,1:T(8,128)S(1)} %convolution_bitcast_fusion.6), channel_id=1, replica_groups=mesh['cell'=8,'seq'=32] {'cell'}, use_global_device_ids=true, to_apply=%region_0.0 | all-reduce | flops 196608 | bytes 1179648 | tf_op jit(solution)/shard_map/psum | solution.py:75
  74.4 5.8 collective-permute-start
  80.2 1.3 collective-permute-start.7
  81.5 1.3 collective-permute-start.6
  82.8 3.3 collective-permute-start.2
  86.1 4.0 collective-permute-start.1
  93.9 5.3 collective-permute-start.3
  100.3 2.1 collective-permute-done.1
  102.3 1.3 collective-permute-start.5
  104.6 1.3 collective-permute-start.4
  108.1 5.0 collective-permute-done.5
  114.2 1.6 fusion.66
  115.7 2.4 copy.86
  118.1 48.4 %while.54 = (s32[]{:T(128)}, f32[256,2]{0,1:T(2,128)S(1)}, f32[256,2]{0,1:T(2,128)S(1)}, s32[]{:T(128)}, bf16[2304,2,128]{2,0,1:T(8,128)(2,1)}, /*index=5*/bf16[...) while((s32[]{:T(128)}, f32[256,2]{0,1:T(2,128)S(1)}, ...), condition=%wide.region_6.7_spmd.clone, body=%wide.region_2.6_spmd.clone.sunk | while | flops 34921744 | bytes 3791994 | solution.py:112
  121.2 1.2 fusion.105
  126.6 1.2 fusion.105
  132.0 1.2 fusion.105
  137.3 1.2 fusion.105
  142.7 1.2 fusion.105
  148.1 1.2 fusion.105
  153.5 1.2 fusion.105
  158.9 1.2 fusion.105
  164.3 1.2 fusion.105
  166.5 51.4 %while.55 = (s32[]{:T(128)}, f32[256,2,128]{0,2,1:T(8,128)}, bf16[2304,2,128]{0,2,1:T(8,128)(2,1)}, s32[]{:T(128)}, bf16[2304,2,128]{2,0,1:T(8,128)(2,1)}, /*ind...) while((s32[]{:T(128)}, f32[256,2,128]{0,2,1:T(8,128)}, ...), condition=%wide.region_9.10_spmd.clone, body=%wide.region_7.9_spmd.clone.sunk | while | flops 68473616 | bytes 3834520 | solution.py:124
  169.9 2.4 fusion.112
  175.5 2.4 fusion.112
  181.2 2.4 fusion.112
  186.9 2.4 fusion.112
  192.7 2.4 fusion.112
  198.4 2.4 fusion.112
  204.1 2.4 fusion.112
  209.8 2.4 fusion.112
  215.5 2.4 fusion.112
  219.0 2.4 broadcast_in_dim.354
  221.4 60.5 %while.56 = (s32[]{:T(128)}, f32[256,2,128]{0,2,1:T(8,128)S(1)}, f32[32,2]{0,1:T(2,128)S(1)}, f32[2304,512]{0,1:T(8,128)}, bf16[2304,2,128]{2,0,1:T(8,128)(2,1)}...) while((s32[]{:T(128)}, f32[256,2,128]{0,2,1:T(8,128)S(1)}, ...), condition=%wide.region_14.15_spmd.clone, body=%wide.region_11.14_spmd.clone.sunk | while | flops 505679744 | bytes 7515830 | solution.py:177
  225.4 1.4 fusion.125
  232.1 1.4 fusion.125
  238.9 1.4 fusion.125
  245.6 1.4 fusion.125
  252.3 1.4 fusion.125
  259.1 1.4 fusion.125
  265.8 1.4 fusion.125
  272.5 1.4 fusion.125
  279.2 1.4 fusion.125
  281.9 2.6 fusion.65
  284.6 1.3 collective-permute-start.8
  285.9 4.4 collective-permute-start.13
  290.3 4.3 collective-permute-start.12
  294.6 1.3 collective-permute-start.11
  295.9 1.3 collective-permute-start.10
  297.2 5.6 collective-permute-done.8
  302.8 1.3 collective-permute-start.9
  304.1 8.0 %collective-permute-done.13 = f32[256,512]{0,1:T(8,128)S(1)} collective-permute-done((f32[256,512]{0,1:T(8,128)S(1)}, f32[256,512]{0,1:T(8,128)S(1)}, u32[]{:S(2)}, u32[]{:S(2)}) %collective-permute-start.13) | collective-permute-done | bytes 524320 | tf_op jit(solution)/shard_map/ppermute | solution.py:16
  312.1 8.6 %collective-permute-start.15 = (f32[256,512]{0,1:T(8,128)S(1)}, f32[256,512]{0,1:T(8,128)S(1)}, u32[]{:S(2)}, u32[]{:S(2)}) collective-permute-start(f32[256,512]{0,1:T(8,128)S(1)} %get-tuple-element.1199), channel_id=1, source_target_pairs={{0,4},{1,5},{2,6},{3,7},{4,8},{5,9},{6,10},{7,11},{8,12},{9,13},{1... | collective-permute-start | bytes 1572872 | tf_op jit(solution)/shard_map/ppermute | solution.py:16
  320.7 3.4 collective-permute-start.14
  324.1 10.8 %collective-permute-done.10 = f32[256,512]{0,1:T(8,128)S(1)} collective-permute-done((f32[256,512]{0,1:T(8,128)S(1)}, f32[256,512]{0,1:T(8,128)S(1)}, u32[]{:S(2)}, u32[]{:S(2)}) %collective-permute-start.10) | collective-permute-done | bytes 524320 | tf_op jit(solution)/shard_map/ppermute | solution.py:16
  335.1 14.4 %collective-permute-done.14 = f32[256,512]{0,1:T(8,128)S(1)} collective-permute-done((f32[256,512]{0,1:T(8,128)S(1)}, f32[256,512]{0,1:T(8,128)S(1)}, u32[]{:S(2)}, u32[]{:S(2)}) %collective-permute-start.14) | collective-permute-done | bytes 524320 | tf_op jit(solution)/shard_map/ppermute | solution.py:16
  349.6 1.4 add_add_fusion
  352.0 123.4 %all-reduce.4.cloned.1.call-done = f32[256,768]{0,1:T(8,128)} async-done(((f32[256,768]{0,1:T(8,128)}), f32[256,768]{0,1:T(8,128)}) %all-reduce.4.cloned.1.call-update) | async-done | bytes 786448 | tf_op jit(solution)/shard_map/psum | solution.py:188
  475.4 2.5 convolution_bitcast_fusion.7
  478.9 77.6 %psum.31 = f32[32,32,2]{1,2,0:T(2,128)} all-reduce(f32[32,32,2]{1,2,0:T(2,128)S(1)} %broadcast_select_fusion.1), channel_id=1, replica_groups=mesh['cell'=8,'seq'=32] {'cell','seq'}, use_global_device_ids=true, to_apply=%region_17.18 | all-reduce | flops 2048 | bytes 16384 | tf_op jit(solution)/shard_map/psum | solution.py:197
  556.4 193.2 %all-reduce.6.cloned.1.call-done = f32[192,768]{1,0:T(8,128)} async-done(((f32[192,768]{1,0:T(8,128)}), f32[192,768]{1,0:T(8,128)}) %all-reduce.6.cloned.1.call-update) | async-done | bytes 589840 | tf_op jit(solution)/shard_map/psum | solution.py:195
  749.6 1.9 copy.153
  (502 shorter events, 126.7 us)
Async XLA Ops:
  7.2 1.7 copy-start
  7.2 83.6 %copy-start.9 = (f32[32,32,2]{1,2,0:T(2,128)S(1)}, f32[32,32,2]{1,2,0:T(2,128)}, u32[]{:S(2)}) copy-start(f32[32,32,2]{1,2,0:T(2,128)} %param.16) | copy-start | bytes 24580
  7.2 86.6 %copy-start.8 = (bf16[1,256,256]{2,1,0:T(8,128)(2,1)S(1)}, bf16[1,256,256]{2,1,0:T(8,128)(2,1)}, u32[]{:S(2)}) copy-start(bf16[1,256,256]{2,1,0:T(8,128)(2,1)} %param.17) | copy-start | bytes 393220
  7.2 468.2 %all-reduce.4.cloned.1.call-start = ((), (), s32[]{:S(2)}) async-start(), calls=%async_computation | async-start | bytes 1572864 | tf_op jit(solution)/shard_map/psum | solution.py:188
  73.3 33.6 %copy-start.5 = (bf16[256,768]{0,1:T(8,128)(2,1)S(1)}, bf16[256,768]{0,1:T(8,128)(2,1)}, u32[]{:S(2)}) copy-start(bf16[256,768]{0,1:T(8,128)(2,1)} %all-reduce.7) | copy-start | bytes 1179652
  74.4 19.6 %collective-permute-start = (bf16[256,512]{0,1:T(8,128)(2,1)S(1)}, bf16[256,512]{0,1:T(8,128)(2,1)}, u32[]{:S(2)}, u32[]{:S(2)}) collective-permute-start(bf16[256,512]{0,1:T(8,128)(2,1)S(1)} %slice.52), channel_id=1, source_target_pairs={{0,4},{1,5},{2,6},{3,7},{4,8},{5,9},{6,10},{7,11},{8,12},{9,13},{1... | collective-permute-start | bytes 786440 | tf_op jit(solution)/shard_map/ppermute | solution.py:16
  80.2 33.9 %collective-permute-start.7 = (bf16[256,512]{0,1:T(8,128)(2,1)S(1)}, bf16[256,512]{0,1:T(8,128)(2,1)S(1)}, u32[]{:S(2)}, u32[]{:S(2)}) collective-permute-start(bf16[256,512]{0,1:T(8,128)(2,1)S(1)} %slice.52), channel_id=1, source_target_pairs={{4,0},{5,1},{6,2},{7,3},{8,4},{9,5},{10,6},{11,7},{12,8},{13,9},{1... | collective-permute-start | bytes 786440 | tf_op jit(solution)/shard_map/ppermute | solution.py:16
  81.5 31.7 %collective-permute-start.6 = (bf16[256,512]{0,1:T(8,128)(2,1)S(1)}, bf16[256,512]{0,1:T(8,128)(2,1)}, u32[]{:S(2)}, u32[]{:S(2)}) collective-permute-start(bf16[256,512]{0,1:T(8,128)(2,1)S(1)} %slice.52), channel_id=1, source_target_pairs={{3,0},{4,1},{5,2},{6,3},{7,4},{8,5},{9,6},{10,7},{11,8},{12,9},{13... | collective-permute-start | bytes 786440 | tf_op jit(solution)/shard_map/ppermute | solution.py:16
  82.8 21.8 %collective-permute-start.2 = (bf16[256,512]{0,1:T(8,128)(2,1)S(1)}, bf16[256,512]{0,1:T(8,128)(2,1)}, u32[]{:S(2)}, u32[]{:S(2)}) collective-permute-start(bf16[256,512]{0,1:T(8,128)(2,1)S(1)} %slice.52), channel_id=1, source_target_pairs={{0,2},{1,3},{2,4},{3,5},{4,6},{5,7},{6,8},{7,9},{8,10},{9,11},{10,... | collective-permute-start | bytes 786440 | tf_op jit(solution)/shard_map/ppermute | solution.py:16
  86.1 16.3 %collective-permute-start.1 = (bf16[256,512]{0,1:T(8,128)(2,1)S(1)}, bf16[256,512]{0,1:T(8,128)(2,1)}, u32[]{:S(2)}, u32[]{:S(2)}) collective-permute-start(bf16[256,512]{0,1:T(8,128)(2,1)S(1)} %slice.52), channel_id=1, source_target_pairs={{0,3},{1,4},{2,5},{3,6},{4,7},{5,8},{6,9},{7,10},{8,11},{9,12},{10... | collective-permute-start | bytes 786440 | tf_op jit(solution)/shard_map/ppermute | solution.py:16
  93.9 12.9 %collective-permute-start.3 = (bf16[256,512]{0,1:T(8,128)(2,1)S(1)}, bf16[256,512]{0,1:T(8,128)(2,1)S(1)}, u32[]{:S(2)}, u32[]{:S(2)}) collective-permute-start(bf16[256,512]{0,1:T(8,128)(2,1)S(1)} %slice.52), channel_id=1, source_target_pairs={{0,1},{1,2},{2,3},{3,4},{4,5},{5,6},{6,7},{7,8},{8,9},{9,10},{10,1... | collective-permute-start | bytes 786440 | tf_op jit(solution)/shard_map/ppermute | solution.py:16
  102.3 10.8 %collective-permute-start.5 = (bf16[256,512]{0,1:T(8,128)(2,1)S(1)}, bf16[256,512]{0,1:T(8,128)(2,1)S(1)}, u32[]{:S(2)}, u32[]{:S(2)}) collective-permute-start(bf16[256,512]{0,1:T(8,128)(2,1)S(1)} %slice.52), channel_id=1, source_target_pairs={{2,0},{3,1},{4,2},{5,3},{6,4},{7,5},{8,6},{9,7},{10,8},{11,9},{12,... | collective-permute-start | bytes 786440 | tf_op jit(solution)/shard_map/ppermute | solution.py:16
  104.6 3.4 collective-permute-start.4
  115.7 2.4 copy-start.7
  166.5 3.3 copy-start.1
  172.2 3.3 copy-start.1
  177.9 3.3 copy-start.1
  183.6 3.3 copy-start.1
  189.4 3.3 copy-start.1
  195.1 3.3 copy-start.1
  200.8 3.3 copy-start.1
  206.5 3.3 copy-start.1
  212.2 3.3 copy-start.1
  218.9 2.5 copy-start.2
  218.9 2.5 copy-start.3
  219.0 2.5 copy-start.4
  219.0 2.5 copy-start.10
  284.6 18.3 %collective-permute-start.8 = (f32[256,512]{0,1:T(8,128)S(1)}, f32[256,512]{0,1:T(8,128)S(1)}, u32[]{:S(2)}, u32[]{:S(2)}) collective-permute-start(f32[256,512]{0,1:T(8,128)S(1)} %get-tuple-element.1193), channel_id=1, source_target_pairs={{4,0},{5,1},{6,2},{7,3},{8,4},{9,5},{10,6},{11,7},{12,8},{13,9},{1... | collective-permute-start | bytes 1572872 | tf_op jit(solution)/shard_map/ppermute | solution.py:16
  285.9 26.2 %collective-permute-start.13 = (f32[256,512]{0,1:T(8,128)S(1)}, f32[256,512]{0,1:T(8,128)S(1)}, u32[]{:S(2)}, u32[]{:S(2)}) collective-permute-start(f32[256,512]{0,1:T(8,128)S(1)} %get-tuple-element.1194), channel_id=1, source_target_pairs={{0,2},{1,3},{2,4},{3,5},{4,6},{5,7},{6,8},{7,9},{8,10},{9,11},{10,... | collective-permute-start | bytes 1572872 | tf_op jit(solution)/shard_map/ppermute | solution.py:16
  290.3 30.4 %collective-permute-start.12 = (f32[256,512]{0,1:T(8,128)S(1)}, f32[256,512]{0,1:T(8,128)S(1)}, u32[]{:S(2)}, u32[]{:S(2)}) collective-permute-start(f32[256,512]{0,1:T(8,128)S(1)} %get-tuple-element.1195), channel_id=1, source_target_pairs={{0,1},{1,2},{2,3},{3,4},{4,5},{5,6},{6,7},{7,8},{8,9},{9,10},{10,1... | collective-permute-start | bytes 1572872 | tf_op jit(solution)/shard_map/ppermute | solution.py:16
  294.6 29.5 %collective-permute-start.11 = (f32[256,512]{0,1:T(8,128)S(1)}, f32[256,512]{0,1:T(8,128)S(1)}, u32[]{:S(2)}, u32[]{:S(2)}) collective-permute-start(f32[256,512]{0,1:T(8,128)S(1)} %get-tuple-element.1196), channel_id=1, source_target_pairs={{1,0},{2,1},{3,2},{4,3},{5,4},{6,5},{7,6},{8,7},{9,8},{10,9},{11,1... | collective-permute-start | bytes 1572872 | tf_op jit(solution)/shard_map/ppermute | solution.py:16
  295.9 39.0 %collective-permute-start.10 = (f32[256,512]{0,1:T(8,128)S(1)}, f32[256,512]{0,1:T(8,128)S(1)}, u32[]{:S(2)}, u32[]{:S(2)}) collective-permute-start(f32[256,512]{0,1:T(8,128)S(1)} %get-tuple-element.1197), channel_id=1, source_target_pairs={{2,0},{3,1},{4,2},{5,3},{6,4},{7,5},{8,6},{9,7},{10,8},{11,9},{12,... | collective-permute-start | bytes 1572872 | tf_op jit(solution)/shard_map/ppermute | solution.py:16
  302.8 32.3 %collective-permute-start.9 = (f32[256,512]{0,1:T(8,128)S(1)}, f32[256,512]{0,1:T(8,128)S(1)}, u32[]{:S(2)}, u32[]{:S(2)}) collective-permute-start(f32[256,512]{0,1:T(8,128)S(1)} %get-tuple-element.1198), channel_id=1, source_target_pairs={{3,0},{4,1},{5,2},{6,3},{7,4},{8,5},{9,6},{10,7},{11,8},{12,9},{13... | collective-permute-start | bytes 1572872 | tf_op jit(solution)/shard_map/ppermute | solution.py:16
  312.1 23.0 %collective-permute-start.15 = (f32[256,512]{0,1:T(8,128)S(1)}, f32[256,512]{0,1:T(8,128)S(1)}, u32[]{:S(2)}, u32[]{:S(2)}) collective-permute-start(f32[256,512]{0,1:T(8,128)S(1)} %get-tuple-element.1199), channel_id=1, source_target_pairs={{0,4},{1,5},{2,6},{3,7},{4,8},{5,9},{6,10},{7,11},{8,12},{9,13},{1... | collective-permute-start | bytes 1572872 | tf_op jit(solution)/shard_map/ppermute | solution.py:16
  320.7 28.9 %collective-permute-start.14 = (f32[256,512]{0,1:T(8,128)S(1)}, f32[256,512]{0,1:T(8,128)S(1)}, u32[]{:S(2)}, u32[]{:S(2)}) collective-permute-start(f32[256,512]{0,1:T(8,128)S(1)} %get-tuple-element.1200), channel_id=1, source_target_pairs={{0,3},{1,4},{2,5},{3,6},{4,7},{5,8},{6,9},{7,10},{8,11},{9,12},{10... | collective-permute-start | bytes 1572872 | tf_op jit(solution)/shard_map/ppermute | solution.py:16
  351.0 124.5 %copy-start.6 = (bf16[256,192]{0,1:T(8,128)(2,1)S(1)}, bf16[256,192]{0,1:T(8,128)(2,1)}, u32[]{:S(2)}) copy-start(bf16[256,192]{0,1:T(8,128)(2,1)} %param.12) | copy-start | bytes 294916
  351.9 397.7 %all-reduce.6.cloned.1.call-start = ((), (), s32[]{:S(2)}) async-start(), calls=%async_computation.1 | async-start | bytes 1179648 | tf_op jit(solution)/shard_map/psum | solution.py:195
Sparse Core Ops, SparseCore 0:
  352.1 123.3 all-reduce.3
  478.6 270.9 all-reduce.5
where the time goes:
time: 761 us; the launch traced here: 758 us
  waiting for transfers between devices  364 us (48%)
  blocking collectives  141 us (19%)
  matrix products  100 us (13%)
  local copies, waits for them, and re-layouts  57.9 us (8%)
  starting transfers between devices  49.5 us (7%)
  other arithmetic  29 us (4%)
  between operations  15.1 us (2%)
    psum x1, waiting for transfers between devices, local(): grad_qkv = lax.psum(share, 'seq')  193 us
    psum x1, waiting for transfers between devices, local(): summed_rows = lax.psum(row_grads, 'cell')  123 us
    psum x1, blocking collectives, local(): grad_table = lax.psum(table_term, ('cell', 'seq'))  77.6 us
    psum x1, blocking collectives, local(): projected = lax.psum(partial_qkv, 'cell').astype(jnp.bfloat16)  63.3 us
    ppermute x16, starting transfers between devices, passed_along(): return lax.ppermute(block, axis, route)  49.5 us
    ppermute x16, waiting for transfers between devices, passed_along(): return lax.ppermute(block, axis, route)  47.2 us
    add x45, local copies, waits for them, and re-layouts, band_scores(): shaped = shaped + bias_terms[:, None]  26.1 us
    dot_general x18, matrix products, band_scores(): jnp.einsum('qhd,khd->qhk', query_rows, key_rows, preferred_element_type=j...  22.1 us
  transfers between devices with their start and end apart: 18, of which 10 were waited for; matrix products, arithmetic and copies ran while one was open for 1% of the time, Pallas kernels for 0%

commit v1 on v0

--- a/solution.py
+++ b/solution.py
@@ -8,6 +8,10 @@
 HD = 128
 TILE = 128
 BT = 16
+
+
+def run_fill(load, shard_axis):
+    return lax.all_gather(load, axis_name=shard_axis).sum(axis=0)
 
 
 def passed_along(block, axis, distance):
@@ -185,7 +189,7 @@
             key_grads = key_grads + return_grads(segment, offset)
     query_grads = (q_total * factor).reshape(row_count, inner_width)
     row_grads = jnp.concatenate([query_grads, key_grads], axis=1)
-    summed_rows = lax.psum(row_grads, "cell")
+    summed_rows = run_fill(row_grads, "cell")
     share = jnp.dot(
         features.astype(jnp.float32).T,
         summed_rows,

time: 761 us -> 804 us (1.057)
  waiting for transfers between devices: 364 us -> 403 us
    all_gather x0 -> x1, waiting for transfers between devices: none -> 165 us  [run_fill(): return lax.all_gather(load, axis_name=shard_axis).sum(axis=0)]
    psum x1 -> x0, waiting for transfers between devices: 123 us -> none  [local(): summed_rows = lax.psum(row_grads, 'cell')]
    unnamed x32 -> x33, local copies, waits for them, and re-layouts: 10.7 us -> 16.5 us
where the time goes in v1:
time: 804 us; the launch traced here: 801 us
  waiting for transfers between devices  403 us (50%)
  blocking collectives  137 us (17%)
  matrix products  99 us (12%)
  local copies, waits for them, and re-layouts  63.8 us (8%)
  starting transfers between devices  49.7 us (6%)
  other arithmetic  31.2 us (4%)
  between operations  15.1 us (2%)
    psum x1, waiting for transfers between devices, local(): grad_qkv = lax.psum(share, 'seq')  191 us
    all_gather x1, waiting for transfers between devices, run_fill(): return lax.all_gather(load, axis_name=shard_axis).sum(axis=0)  165 us
    psum x1, blocking collectives, local(): grad_table = lax.psum(table_term, ('cell', 'seq'))  73.6 us
    psum x1, blocking collectives, local(): projected = lax.psum(partial_qkv, 'cell').astype(jnp.bfloat16)  63.3 us
    ppermute x16, starting transfers between devices, passed_along(): return lax.ppermute(block, axis, route)  49.4 us
    ppermute x16, waiting for transfers between devices, passed_along(): return lax.ppermute(block, axis, route)  47.3 us
    add x45, local copies, waits for them, and re-layouts, band_scores(): shaped = shaped + bias_terms[:, None]  26.1 us
    dot_general x18, matrix products, band_scores(): jnp.einsum('qhd,khd->qhk', query_rows, key_rows, preferred_element_type=j...  22.1 us
  transfers between devices with their start and end apart: 18, of which 10 were waited for; matrix products, arithmetic and copies ran while one was open for 1% of the time, Pallas kernels for 0%

profile of v1, /device:TPU:2, one launch (start us, length us, event | category | flops | bytes accessed | tf_op | source)
XLA Modules:
  0.0 800.9 jit_solution(9805088638674234868)
XLA Ops:
  7.3 1.6 copy-done
  10.0 63.3 %all-reduce.4 = bf16[256,768]{0,1:T(8,128)(2,1)} all-reduce(f32[256,768]{0,1:T(8,128)S(1)} %convolution_bitcast_fusion.6), channel_id=1, replica_groups=mesh['cell'=8,'seq'=32] {'cell'}, use_global_device_ids=true, to_apply=%region_0.0 | all-reduce | flops 196608 | bytes 1179648 | tf_op jit(solution)/shard_map/psum | solution.py:79
  74.4 5.8 collective-permute-start
  80.2 1.3 collective-permute-start.7
  81.5 1.3 collective-permute-start.6
  82.8 3.3 collective-permute-start.2
  86.0 4.0 collective-permute-start.1
  93.9 5.3 collective-permute-start.3
  100.2 2.1 collective-permute-done.1
  102.3 1.3 collective-permute-start.5
  104.6 1.3 collective-permute-start.4
  108.1 5.0 collective-permute-done.5
  114.1 1.6 fusion.66
  115.7 2.4 copy.86
  118.1 48.4 %while.54 = (s32[]{:T(128)}, f32[256,2]{0,1:T(2,128)S(1)}, f32[256,2]{0,1:T(2,128)S(1)}, s32[]{:T(128)}, bf16[2304,2,128]{2,0,1:T(8,128)(2,1)}, /*index=5*/bf16[...) while((s32[]{:T(128)}, f32[256,2]{0,1:T(2,128)S(1)}, ...), condition=%wide.region_6.7_spmd.clone, body=%wide.region_2.6_spmd.clone.sunk | while | flops 34921744 | bytes 3791994 | solution.py:116
  121.2 1.2 fusion.105
  126.6 1.2 fusion.105
  132.0 1.2 fusion.105
  137.3 1.2 fusion.105
  142.7 1.2 fusion.105
  148.1 1.2 fusion.105
  153.5 1.2 fusion.105
  166.5 51.4 %while.55 = (s32[]{:T(128)}, f32[256,2,128]{0,2,1:T(8,128)}, bf16[2304,2,128]{0,2,1:T(8,128)(2,1)}, s32[]{:T(128)}, bf16[2304,2,128]{2,0,1:T(8,128)(2,1)}, /*ind...) while((s32[]{:T(128)}, f32[256,2,128]{0,2,1:T(8,128)}, ...), condition=%wide.region_9.10_spmd.clone, body=%wide.region_7.9_spmd.clone.sunk | while | flops 68473616 | bytes 3834520 | solution.py:128
  169.9 2.4 fusion.112
  175.5 2.4 fusion.112
  181.2 2.4 fusion.112
  186.9 2.4 fusion.112
  192.7 2.4 fusion.112
  198.4 2.4 fusion.112
  204.1 2.4 fusion.112
  209.8 2.4 fusion.112
  215.5 2.4 fusion.112
  219.0 2.4 broadcast_in_dim.354
  221.4 60.5 %while.56 = (s32[]{:T(128)}, f32[256,2,128]{0,2,1:T(8,128)S(1)}, f32[32,2]{0,1:T(2,128)S(1)}, f32[2304,512]{0,1:T(8,128)}, bf16[2304,2,128]{2,0,1:T(8,128)(2,1)}...) while((s32[]{:T(128)}, f32[256,2,128]{0,2,1:T(8,128)S(1)}, ...), condition=%wide.region_14.15_spmd.clone, body=%wide.region_11.14_spmd.clone.sunk | while | flops 505679744 | bytes 7515830 | solution.py:181
  225.4 1.4 fusion.125
  232.1 1.4 fusion.125
  238.9 1.4 fusion.125
  245.6 1.4 fusion.125
  252.3 1.4 fusion.125
  259.1 1.4 fusion.125
  265.8 1.4 fusion.125
  272.5 1.4 fusion.125
  279.2 1.4 fusion.125
  281.9 2.6 fusion.65
  284.6 1.3 collective-permute-start.8
  285.9 4.4 collective-permute-start.13
  290.3 4.3 collective-permute-start.12
  294.6 1.3 collective-permute-start.11
  295.9 1.3 collective-permute-start.10
  297.2 5.6 collective-permute-done.8
  302.8 1.3 collective-permute-start.9
  304.1 8.0 collective-permute-done.13
  312.1 8.6 %collective-permute-start.15 = (f32[256,512]{0,1:T(8,128)S(1)}, f32[256,512]{0,1:T(8,128)S(1)}, u32[]{:S(2)}, u32[]{:S(2)}) collective-permute-start(f32[256,512]{0,1:T(8,128)S(1)} %get-tuple-element.1199), channel_id=1, source_target_pairs={{0,4},{1,5},{2,6},{3,7},{4,8},{5,9},{6,10},{7,11},{8,12},{9,13},{1... | collective-permute-start | bytes 1572872 | tf_op jit(solution)/shard_map/ppermute | solution.py:20
  320.7 3.4 collective-permute-start.14
  324.1 10.8 %collective-permute-done.10 = f32[256,512]{0,1:T(8,128)S(1)} collective-permute-done((f32[256,512]{0,1:T(8,128)S(1)}, f32[256,512]{0,1:T(8,128)S(1)}, u32[]{:S(2)}, u32[]{:S(2)}) %collective-permute-start.10) | collective-permute-done | bytes 524320 | tf_op jit(solution)/shard_map/ppermute | solution.py:20
  335.2 14.4 %collective-permute-done.14 = f32[256,512]{0,1:T(8,128)S(1)} collective-permute-done((f32[256,512]{0,1:T(8,128)S(1)}, f32[256,512]{0,1:T(8,128)S(1)}, u32[]{:S(2)}, u32[]{:S(2)}) %collective-permute-start.14) | collective-permute-done | bytes 524320 | tf_op jit(solution)/shard_map/ppermute | solution.py:20
  349.6 1.4 add_add_fusion
  352.1 164.8 %all-gather.3.cloned.1.call-done = f32[2048,768]{0,1:T(8,128)} async-done(((f32[256,768]{0,1:T(8,128)}), f32[2048,768]{0,1:T(8,128)}) %all-gather.3.cloned.1.call-update) | async-done | bytes 6291472 | tf_op jit(solution)/shard_map/all_gather | solution.py:14
  517.0 5.8 copy.98
  522.8 2.2 bitcast_reduce_fusion.1
  525.0 1.4 convolution_bitcast_fusion.7
  527.3 73.6 %psum.23 = f32[32,32,2]{1,2,0:T(2,128)} all-reduce(f32[32,32,2]{1,2,0:T(2,128)S(1)} %broadcast_select_fusion.1), channel_id=1, replica_groups=mesh['cell'=8,'seq'=32] {'cell','seq'}, use_global_device_ids=true, to_apply=%region_17.18 | all-reduce | flops 2048 | bytes 16384 | tf_op jit(solution)/shard_map/psum | solution.py:201
  600.9 191.3 %all-reduce.3.cloned.1.call-done = f32[192,768]{1,0:T(8,128)} async-done(((f32[192,768]{1,0:T(8,128)}), f32[192,768]{1,0:T(8,128)}) %all-reduce.3.cloned.1.call-update) | async-done | bytes 589840 | tf_op jit(solution)/shard_map/psum | solution.py:199
  792.1 1.9 copy.153
  (504 shorter events, 129.3 us)
Async XLA Ops:
  7.2 1.7 copy-start
  7.2 83.5 %copy-start.9 = (f32[32,32,2]{1,2,0:T(2,128)S(1)}, f32[32,32,2]{1,2,0:T(2,128)}, u32[]{:S(2)}) copy-start(f32[32,32,2]{1,2,0:T(2,128)} %param.16) | copy-start | bytes 24580
  7.2 86.6 %copy-start.8 = (bf16[1,256,256]{2,1,0:T(8,128)(2,1)S(1)}, bf16[1,256,256]{2,1,0:T(8,128)(2,1)}, u32[]{:S(2)}) copy-start(bf16[1,256,256]{2,1,0:T(8,128)(2,1)} %param.17) | copy-start | bytes 393220
  7.2 509.8 %all-gather.3.cloned.1.call-start = ((), (), s32[]{:S(2)}) async-start(), calls=%async_computation.1 | async-start | bytes 7077888 | tf_op jit(solution)/shard_map/all_gather | solution.py:14
  73.3 33.6 %copy-start.5 = (bf16[256,768]{0,1:T(8,128)(2,1)S(1)}, bf16[256,768]{0,1:T(8,128)(2,1)}, u32[]{:S(2)}) copy-start(bf16[256,768]{0,1:T(8,128)(2,1)} %all-reduce.4) | copy-start | bytes 1179652
  74.4 19.5 %collective-permute-start = (bf16[256,512]{0,1:T(8,128)(2,1)S(1)}, bf16[256,512]{0,1:T(8,128)(2,1)}, u32[]{:S(2)}, u32[]{:S(2)}) collective-permute-start(bf16[256,512]{0,1:T(8,128)(2,1)S(1)} %slice.52), channel_id=1, source_target_pairs={{0,4},{1,5},{2,6},{3,7},{4,8},{5,9},{6,10},{7,11},{8,12},{9,13},{1... | collective-permute-start | bytes 786440 | tf_op jit(solution)/shard_map/ppermute | solution.py:20
  80.2 33.9 %collective-permute-start.7 = (bf16[256,512]{0,1:T(8,128)(2,1)S(1)}, bf16[256,512]{0,1:T(8,128)(2,1)S(1)}, u32[]{:S(2)}, u32[]{:S(2)}) collective-permute-start(bf16[256,512]{0,1:T(8,128)(2,1)S(1)} %slice.52), channel_id=1, source_target_pairs={{4,0},{5,1},{6,2},{7,3},{8,4},{9,5},{10,6},{11,7},{12,8},{13,9},{1... | collective-permute-start | bytes 786440 | tf_op jit(solution)/shard_map/ppermute | solution.py:20
  81.5 31.7 %collective-permute-start.6 = (bf16[256,512]{0,1:T(8,128)(2,1)S(1)}, bf16[256,512]{0,1:T(8,128)(2,1)}, u32[]{:S(2)}, u32[]{:S(2)}) collective-permute-start(bf16[256,512]{0,1:T(8,128)(2,1)S(1)} %slice.52), channel_id=1, source_target_pairs={{3,0},{4,1},{5,2},{6,3},{7,4},{8,5},{9,6},{10,7},{11,8},{12,9},{13... | collective-permute-start | bytes 786440 | tf_op jit(solution)/shard_map/ppermute | solution.py:20
  82.8 21.8 %collective-permute-start.2 = (bf16[256,512]{0,1:T(8,128)(2,1)S(1)}, bf16[256,512]{0,1:T(8,128)(2,1)}, u32[]{:S(2)}, u32[]{:S(2)}) collective-permute-start(bf16[256,512]{0,1:T(8,128)(2,1)S(1)} %slice.52), channel_id=1, source_target_pairs={{0,2},{1,3},{2,4},{3,5},{4,6},{5,7},{6,8},{7,9},{8,10},{9,11},{10,... | collective-permute-start | bytes 786440 | tf_op jit(solution)/shard_map/ppermute | solution.py:20
  86.0 16.3 %collective-permute-start.1 = (bf16[256,512]{0,1:T(8,128)(2,1)S(1)}, bf16[256,512]{0,1:T(8,128)(2,1)}, u32[]{:S(2)}, u32[]{:S(2)}) collective-permute-start(bf16[256,512]{0,1:T(8,128)(2,1)S(1)} %slice.52), channel_id=1, source_target_pairs={{0,3},{1,4},{2,5},{3,6},{4,7},{5,8},{6,9},{7,10},{8,11},{9,12},{10... | collective-permute-start | bytes 786440 | tf_op jit(solution)/shard_map/ppermute | solution.py:20
  93.9 13.0 %collective-permute-start.3 = (bf16[256,512]{0,1:T(8,128)(2,1)S(1)}, bf16[256,512]{0,1:T(8,128)(2,1)S(1)}, u32[]{:S(2)}, u32[]{:S(2)}) collective-permute-start(bf16[256,512]{0,1:T(8,128)(2,1)S(1)} %slice.52), channel_id=1, source_target_pairs={{0,1},{1,2},{2,3},{3,4},{4,5},{5,6},{6,7},{7,8},{8,9},{9,10},{10,1... | collective-permute-start | bytes 786440 | tf_op jit(solution)/shard_map/ppermute | solution.py:20
  102.3 10.8 %collective-permute-start.5 = (bf16[256,512]{0,1:T(8,128)(2,1)S(1)}, bf16[256,512]{0,1:T(8,128)(2,1)S(1)}, u32[]{:S(2)}, u32[]{:S(2)}) collective-permute-start(bf16[256,512]{0,1:T(8,128)(2,1)S(1)} %slice.52), channel_id=1, source_target_pairs={{2,0},{3,1},{4,2},{5,3},{6,4},{7,5},{8,6},{9,7},{10,8},{11,9},{12,... | collective-permute-start | bytes 786440 | tf_op jit(solution)/shard_map/ppermute | solution.py:20
  104.6 3.4 collective-permute-start.4
  115.7 2.4 copy-start.7
  166.5 3.3 copy-start.1
  172.2 3.3 copy-start.1
  177.9 3.3 copy-start.1
  183.6 3.3 copy-start.1
  189.4 3.3 copy-start.1
  195.1 3.3 copy-start.1
  200.8 3.3 copy-start.1
  206.5 3.3 copy-start.1
  212.2 3.3 copy-start.1
  218.9 2.5 copy-start.2
  218.9 2.5 copy-start.3
  218.9 2.5 copy-start.4
  219.0 2.5 copy-start.10
  284.6 18.3 %collective-permute-start.8 = (f32[256,512]{0,1:T(8,128)S(1)}, f32[256,512]{0,1:T(8,128)S(1)}, u32[]{:S(2)}, u32[]{:S(2)}) collective-permute-start(f32[256,512]{0,1:T(8,128)S(1)} %get-tuple-element.1193), channel_id=1, source_target_pairs={{4,0},{5,1},{6,2},{7,3},{8,4},{9,5},{10,6},{11,7},{12,8},{13,9},{1... | collective-permute-start | bytes 1572872 | tf_op jit(solution)/shard_map/ppermute | solution.py:20
  285.9 26.2 %collective-permute-start.13 = (f32[256,512]{0,1:T(8,128)S(1)}, f32[256,512]{0,1:T(8,128)S(1)}, u32[]{:S(2)}, u32[]{:S(2)}) collective-permute-start(f32[256,512]{0,1:T(8,128)S(1)} %get-tuple-element.1194), channel_id=1, source_target_pairs={{0,2},{1,3},{2,4},{3,5},{4,6},{5,7},{6,8},{7,9},{8,10},{9,11},{10,... | collective-permute-start | bytes 1572872 | tf_op jit(solution)/shard_map/ppermute | solution.py:20
  290.3 30.4 %collective-permute-start.12 = (f32[256,512]{0,1:T(8,128)S(1)}, f32[256,512]{0,1:T(8,128)S(1)}, u32[]{:S(2)}, u32[]{:S(2)}) collective-permute-start(f32[256,512]{0,1:T(8,128)S(1)} %get-tuple-element.1195), channel_id=1, source_target_pairs={{0,1},{1,2},{2,3},{3,4},{4,5},{5,6},{6,7},{7,8},{8,9},{9,10},{10,1... | collective-permute-start | bytes 1572872 | tf_op jit(solution)/shard_map/ppermute | solution.py:20
  294.6 29.5 %collective-permute-start.11 = (f32[256,512]{0,1:T(8,128)S(1)}, f32[256,512]{0,1:T(8,128)S(1)}, u32[]{:S(2)}, u32[]{:S(2)}) collective-permute-start(f32[256,512]{0,1:T(8,128)S(1)} %get-tuple-element.1196), channel_id=1, source_target_pairs={{1,0},{2,1},{3,2},{4,3},{5,4},{6,5},{7,6},{8,7},{9,8},{10,9},{11,1... | collective-permute-start | bytes 1572872 | tf_op jit(solution)/shard_map/ppermute | solution.py:20
  295.9 39.0 %collective-permute-start.10 = (f32[256,512]{0,1:T(8,128)S(1)}, f32[256,512]{0,1:T(8,128)S(1)}, u32[]{:S(2)}, u32[]{:S(2)}) collective-permute-start(f32[256,512]{0,1:T(8,128)S(1)} %get-tuple-element.1197), channel_id=1, source_target_pairs={{2,0},{3,1},{4,2},{5,3},{6,4},{7,5},{8,6},{9,7},{10,8},{11,9},{12,... | collective-permute-start | bytes 1572872 | tf_op jit(solution)/shard_map/ppermute | solution.py:20
  302.8 32.3 %collective-permute-start.9 = (f32[256,512]{0,1:T(8,128)S(1)}, f32[256,512]{0,1:T(8,128)S(1)}, u32[]{:S(2)}, u32[]{:S(2)}) collective-permute-start(f32[256,512]{0,1:T(8,128)S(1)} %get-tuple-element.1198), channel_id=1, source_target_pairs={{3,0},{4,1},{5,2},{6,3},{7,4},{8,5},{9,6},{10,7},{11,8},{12,9},{13... | collective-permute-start | bytes 1572872 | tf_op jit(solution)/shard_map/ppermute | solution.py:20
  312.1 23.1 %collective-permute-start.15 = (f32[256,512]{0,1:T(8,128)S(1)}, f32[256,512]{0,1:T(8,128)S(1)}, u32[]{:S(2)}, u32[]{:S(2)}) collective-permute-start(f32[256,512]{0,1:T(8,128)S(1)} %get-tuple-element.1199), channel_id=1, source_target_pairs={{0,4},{1,5},{2,6},{3,7},{4,8},{5,9},{6,10},{7,11},{8,12},{9,13},{1... | collective-permute-start | bytes 1572872 | tf_op jit(solution)/shard_map/ppermute | solution.py:20
  320.7 28.9 %collective-permute-start.14 = (f32[256,512]{0,1:T(8,128)S(1)}, f32[256,512]{0,1:T(8,128)S(1)}, u32[]{:S(2)}, u32[]{:S(2)}) collective-permute-start(f32[256,512]{0,1:T(8,128)S(1)} %get-tuple-element.1200), channel_id=1, source_target_pairs={{0,3},{1,4},{2,5},{3,6},{4,7},{5,8},{6,9},{7,10},{8,11},{9,12},{10... | collective-permute-start | bytes 1572872 | tf_op jit(solution)/shard_map/ppermute | solution.py:20
  351.9 440.2 %all-reduce.3.cloned.1.call-start = ((), (), s32[]{:S(2)}) async-start(), calls=%async_computation | async-start | bytes 1179648 | tf_op jit(solution)/shard_map/psum | solution.py:199
  522.8 2.2 copy-start.6
Sparse Core Ops, SparseCore 0:
  352.0 164.8 all-gather.2
  526.5 265.5 all-reduce.2
